TPU v7x, 512 devices: a whole 4x4x16 slice. The times are simulated.
512 devices in a mesh: src: 64 (over z_hi, y, x, core), fac: 8 (over z_lo).
Axes of the slice: x: 4, y: 4, z: 16 (z_hi: 2, z_lo: 8; z = z_hi * 8 + z_lo), core: 2. Of those that a mesh axis runs over, the one named last changes fastest.
Arguments:
- lower_inverse: bfloat16 [8, 1024, 2, 1024], P('fac', 'src'), as said below
- coupling: bfloat16 [8, 1024, 2, 1024], P('fac', 'src'), as said below
- source_cell: int32 [8192], P('src'), may hold values from 0 to 8191
- source_wave: float32 [8192, 2], P('src'), may hold values from -6 to 6
- inflow_field: bfloat16 [8192, 2, 1024], P('src'), may hold values from -6 to 6
- receiver_cell: int32 [8192, 128], P('src'), may hold values from 0 to 8191
- observed: float32 [8192, 2, 128], P('src'), may hold values from -6 to 6
- adjoint: bfloat16 [8192, 8, 2, 1024], P('src', 'fac'), may hold values from -16 to 16
Outputs:
- wavefield: float32 [8192, 8, 2, 1024], P('src', 'fac')
- data_residual: float32 [8192, 2, 128], P('src')
- gradient: float32 [8, 1024], P('fac', 'src')
Inputs may be any that keep to these rules, and one draw needn't show every extreme that they name: lower_inverse[i, j, p, k] is zero where k > j. coupling[i, j, p, k] is zero where k < j.
All inputs are finite; a program needn't handle non-finite values.
Results may differ from a plain program's by a relative error of at most 0.025.
Values may be sent and summed in bfloat16 or wider, within the bound.
No kernel may reach another device: no remote copies, remote signals or barrier semaphores. Data moves between devices by JAX's collectives and lax.ppermute only.
A program may use at most 64 MiB of HBM per device.

v0:
```python
import math
import jax
import jax.numpy as jnp
from jax import lax
from jax.sharding import PartitionSpec as P


def from_behind(shard, axis, by):
    size = lax.axis_size(axis)
    pairs = [(i, i + by) for i in range(size) if 0 <= i + by < size]
    return lax.ppermute(shard, axis, pairs)


def complex_apply(vector, matrix):
    width = matrix.shape[0]
    joined = matrix.reshape(width, 2 * width)
    real_row = jnp.concatenate([vector[:, 0], -vector[:, 1]], axis=1)
    imag_row = jnp.concatenate([vector[:, 1], vector[:, 0]], axis=1)
    stacked = jnp.stack([real_row, imag_row], axis=1).reshape(-1, 2 * width)
    contract_dims = (((1,), (1,)), ((), ()))
    result = lax.dot_general(stacked, joined, contract_dims, preferred_element_type=jnp.float32)
    return result.reshape(vector.shape[0], 2, width)


def source_block(cells, wave, owner, width):
    cell_ids = owner * width + lax.broadcasted_iota(jnp.int32, (width,), 0)
    hit = cells[:, None] == cell_ids[None, :]
    return jnp.where(hit[:, None, :], wave[:, :, None], jnp.zeros((), jnp.float32))


def block_solve(previous, cells, wave, owner, lower_full, coupling_full):
    width = lower_full.shape[0]
    term = source_block(cells, wave, owner, width)
    reduced = (term - complex_apply(previous, coupling_full)).astype(jnp.bfloat16)
    return complex_apply(reduced, lower_full)


def per_device(
    lower_inverse,
    coupling,
    source_cell,
    source_wave,
    inflow_field,
    receiver_cell,
    observed,
    adjoint,
):
    owner = lax.axis_index("fac")
    fac_count = lax.axis_size("fac")
    width = lower_inverse.shape[3]
    sources = source_cell.shape[0]
    whole_lower, whole_coupling = (
        lax.all_gather(lower_inverse, "src", axis=1, tiled=True),
        lax.all_gather(coupling, "src", axis=1, tiled=True),
    )
    lower_full = whole_lower[0]
    coupling_full = whole_coupling[0]
    empty_field = jnp.zeros((sources, 2, width), jnp.float32)

    def section_step(section, carry):
        current, received = carry

        def compute():
            return block_solve(received, source_cell, source_wave, owner, lower_full, coupling_full)

        def unchanged():
            return current

        current = lax.cond(section == owner, compute, unchanged)
        received = from_behind(current.astype(jnp.bfloat16), "fac", 1)
        return (current, received)

    current, received = lax.fori_loop(0, fac_count, section_step, (empty_field, inflow_field))
    local_ids = receiver_cell - owner * width
    inside = (local_ids >= 0) & (local_ids < width)
    clipped = jnp.clip(local_ids, 0, width - 1)
    index_both = jnp.broadcast_to(clipped[:, None, :], observed.shape)
    values = jnp.take_along_axis(current, index_both, axis=2)
    values = jnp.where(inside[:, None, :], values, jnp.zeros((), jnp.float32))
    picked = lax.psum(values.astype(jnp.bfloat16), "fac").astype(jnp.float32)
    scale = 1.0 / math.sqrt(sources * lax.axis_size("src"))
    terms = jnp.sum(current * adjoint[:, 0].astype(jnp.float32), axis=(0, 1)) * scale
    gradient = lax.psum_scatter(terms[None, :], "src", scatter_dimension=1, tiled=True)
    return (current[:, None], picked - observed, gradient)


def solution(mesh):
    placed = (
        P("fac", "src", None, None),
        P("fac", "src", None, None),
        P("src"),
        P("src", None),
        P("src", None, None),
        P("src", None),
        P("src", None, None),
        P("src", "fac", None, None),
    )
    return jax.shard_map(
        per_device,
        mesh=mesh,
        in_specs=placed,
        out_specs=(P("src", "fac", None, None), P("src", None, None), P("fac", "src")),
        check_vma=False,
    )
```

profile of v0, /device:TPU:2, one launch (start us, length us, event | category | flops | bytes accessed | tf_op | source)
XLA Modules:
  0.0 1569.2 jit_solution(6800192813153071421)
XLA Ops:
  7.2 0.7 all-gather.5.cloned.1.call-update
  7.9 0.7 all-gather.3.cloned.1.call-update
  8.7 1.1 copy.19
  9.9 0.9 broadcast_add_fusion
  10.7 0.9 compare_and_fusion
  11.6 0.2 shift-left_or_fusion
  11.8 137.0 %all-gather.5.cloned.1.call-done = bf16[1,1024,2,1024]{3,2,0,1:T(2,128)(2,1)} async-done(((bf16[1,16,2,1024]{3,2,0,1:T(2,128)(2,1)}), bf16[1,1024,2,1024]{3,2,0,1:T(2,128)(2,1)}) %all-gather.5.cloned.1.call-update) | async-done | bytes 4194320 | tf_op jit(solution)/shard_map/all_gather | solution.py:53
  148.8 127.0 %all-gather.3.cloned.1.call-done = bf16[1,1024,2,1024]{3,2,0,1:T(2,128)(2,1)} async-done(((bf16[1,16,2,1024]{3,2,0,1:T(2,128)(2,1)}), bf16[1,1024,2,1024]{3,2,0,1:T(2,128)(2,1)}) %all-gather.3.cloned.1.call-update) | async-done | bytes 4194320 | tf_op jit(solution)/shard_map/all_gather | solution.py:54
  275.8 0.1 broadcast_in_dim.64
  275.9 221.2 %while.18 = (s32[]{:T(128)}, f32[128,2,1024]{2,0,1:T(8,128)S(1)}, bf16[128,2,1024]{2,0,1:T(8,128)(2,1)S(1)}, s32[]{:T(128)}, s32[128]{0:T(128)}, /*index=5*/f32[...) while((s32[]{:T(128)}, f32[128,2,1024]{2,0,1:T(8,128)S(1)}, ...), condition=%wide.region_3.4_spmd, body=%wide.region_0.3_spmd.sunk | while | flops 2154169344 | bytes 39597816 | solution.py:73
  275.9 23.8 %conditional.2 = (f32[128,2,1024]{2,0,1:T(8,128)S(1)}) conditional(s32[]{:T(128)} %convert_element_type.39, f32[128,2,1024]{2,0,1:T(8,128)S(1)} %get-tuple-element.280, (s32[128]{0:T(128)}, s32[]{:T(128)}, f32[128,2]{0,1:T(2,128)}, bf16[128,2,1024]{2,0,1:T(8,128)(2,1)S(1)}, bf16[1,1024,2,1024]{3,2,1,0:T(2,128)(2,1)}, ...), branch_computations={%region_1.0_spmd, %region_2.2_spmd} | conditional | flops 2153907200 | bytes 35927604 | solution.py:69
  276.0 0.8 broadcast_compare_fusion
  276.9 0.1 maximum_bitcast_fusion
  277.0 7.8 reshape.71
  284.8 3.5 fusion
  288.3 0.1 maximum_bitcast_fusion.2
  288.4 7.8 reshape.72
  296.3 3.5 fusion.4
  299.7 0.1 convert_element_type.40
  299.8 1.3 collective-permute-start
  301.1 11.8 collective-permute-done
  313.0 0.1 convert_element_type.40
  313.1 28.2 %collective-permute-start = (bf16[128,2,1024]{2,0,1:T(8,128)(2,1)S(1)}, bf16[128,2,1024]{2,0,1:T(8,128)(2,1)S(1)}, u32[]{:S(2)}, u32[]{:S(2)}) collective-permute-start(bf16[128,2,1024]{2,0,1:T(8,128)(2,1)S(1)} %convert_element_type.40), channel_id=1, source_target_pairs={{0,1},{1,2},{2,3},{3,4},{4,5},{5,6},{6,7},{8,9},{9,10},{10,11},{11... | collective-permute-start | bytes 1572872 | tf_op jit(solution)/shard_map/while/body/eval_jaxpr/ppermute | solution.py:11
  341.3 11.1 collective-permute-done
  352.3 0.1 convert_element_type.40
  352.4 4.4 collective-permute-start
  356.8 10.2 collective-permute-done
  367.1 26.3 %collective-permute-start = (bf16[128,2,1024]{2,0,1:T(8,128)(2,1)S(1)}, bf16[128,2,1024]{2,0,1:T(8,128)(2,1)S(1)}, u32[]{:S(2)}, u32[]{:S(2)}) collective-permute-start(bf16[128,2,1024]{2,0,1:T(8,128)(2,1)S(1)} %convert_element_type.40), channel_id=1, source_target_pairs={{0,1},{1,2},{2,3},{3,4},{4,5},{5,6},{6,7},{8,9},{9,10},{10,11},{11... | collective-permute-start | bytes 1572872 | tf_op jit(solution)/shard_map/while/body/eval_jaxpr/ppermute | solution.py:11
  393.4 9.6 collective-permute-done
  403.0 4.4 collective-permute-start
  407.5 8.6 collective-permute-done
  416.2 26.6 %collective-permute-start = (bf16[128,2,1024]{2,0,1:T(8,128)(2,1)S(1)}, bf16[128,2,1024]{2,0,1:T(8,128)(2,1)S(1)}, u32[]{:S(2)}, u32[]{:S(2)}) collective-permute-start(bf16[128,2,1024]{2,0,1:T(8,128)(2,1)S(1)} %convert_element_type.40), channel_id=1, source_target_pairs={{0,1},{1,2},{2,3},{3,4},{4,5},{5,6},{6,7},{8,9},{9,10},{10,11},{11... | collective-permute-start | bytes 1572872 | tf_op jit(solution)/shard_map/while/body/eval_jaxpr/ppermute | solution.py:11
  442.7 8.0 collective-permute-done
  450.8 0.1 convert_element_type.40
  450.8 4.4 collective-permute-start
  455.3 7.1 collective-permute-done
  462.3 0.1 convert_element_type.40
  462.4 28.0 %collective-permute-start = (bf16[128,2,1024]{2,0,1:T(8,128)(2,1)S(1)}, bf16[128,2,1024]{2,0,1:T(8,128)(2,1)S(1)}, u32[]{:S(2)}, u32[]{:S(2)}) collective-permute-start(bf16[128,2,1024]{2,0,1:T(8,128)(2,1)S(1)} %convert_element_type.40), channel_id=1, source_target_pairs={{0,1},{1,2},{2,3},{3,4},{4,5},{5,6},{6,7},{8,9},{9,10},{10,11},{11... | collective-permute-start | bytes 1572872 | tf_op jit(solution)/shard_map/while/body/eval_jaxpr/ppermute | solution.py:11
  490.5 6.6 collective-permute-done
  497.1 310.7 %gather_fusion = bf16[32768]{0:T(1024)(128)(2,1)S(1)} fusion(f32[128,2,1024]{2,0,1:T(8,128)S(1)} %get-tuple-element.168, s32[32768]{0:T(1024)S(1)} %bitcast.40), kind=kCustom, calls=%fused_computation | custom fusion | bytes 524288 | tf_op jit(solution)/shard_map/jit(take_along_axis)/gather | solution.py:78
  807.8 0.2 fusion.12
  808.0 1.0 copy.24
  809.2 0.9 fusion.14
  810.0 1.8 copy.28
  811.8 624.0 %reduce-scatter.4.cloned.1.call-done = f32[16,1]{1,0:T(8,128)} async-done(((f32[1024,1]{1,0:T(8,128)}), f32[16,1]{1,0:T(8,128)}) %reduce-scatter.4.cloned.1.call-update) | async-done | bytes 80
  1435.8 1.3 copy.25
  1437.1 124.1 %all-reduce.2.cloned.1.call-done = bf16[128,2,128]{2,1,0:T(2,128)(2,1)} async-done(((bf16[128,2,128]{2,1,0:T(2,128)(2,1)}), bf16[128,2,128]{2,1,0:T(2,128)(2,1)}) %all-reduce.2.cloned.1.call-update) | async-done | bytes 65552 | tf_op jit(solution)/shard_map/psum | solution.py:80
  1561.2 1.5 convert_subtract_fusion
  (28 shorter events, 0.5 us)
Async XLA Ops:
  7.2 141.7 %all-gather.5.cloned.1.call-start = ((), (), s32[]{:S(2)}) async-start(), calls=%async_computation.2 | async-start | bytes 4259840 | tf_op jit(solution)/shard_map/all_gather | solution.py:53
  7.9 267.9 %all-gather.3.cloned.1.call-start = ((), (), s32[]{:S(2)}) async-start(), calls=%async_computation.1 | async-start | bytes 4259840 | tf_op jit(solution)/shard_map/all_gather | solution.py:54
  8.6 1427.2 %reduce-scatter.4.cloned.1.call-start = ((), (), s32[]{:S(2)}) async-start(), calls=%async_computation.4 | async-start | bytes 532480
  276.9 7.8 copy-start.2
  299.8 13.2 collective-permute-start
  313.1 39.2 %collective-permute-start = (bf16[128,2,1024]{2,0,1:T(8,128)(2,1)S(1)}, bf16[128,2,1024]{2,0,1:T(8,128)(2,1)S(1)}, u32[]{:S(2)}, u32[]{:S(2)}) collective-permute-start(bf16[128,2,1024]{2,0,1:T(8,128)(2,1)S(1)} %convert_element_type.40), channel_id=1, source_target_pairs={{0,1},{1,2},{2,3},{3,4},{4,5},{5,6},{6,7},{8,9},{9,10},{10,11},{11... | collective-permute-start | bytes 1572872 | tf_op jit(solution)/shard_map/while/body/eval_jaxpr/ppermute | solution.py:11
  352.4 14.6 collective-permute-start
  367.1 35.9 %collective-permute-start = (bf16[128,2,1024]{2,0,1:T(8,128)(2,1)S(1)}, bf16[128,2,1024]{2,0,1:T(8,128)(2,1)S(1)}, u32[]{:S(2)}, u32[]{:S(2)}) collective-permute-start(bf16[128,2,1024]{2,0,1:T(8,128)(2,1)S(1)} %convert_element_type.40), channel_id=1, source_target_pairs={{0,1},{1,2},{2,3},{3,4},{4,5},{5,6},{6,7},{8,9},{9,10},{10,11},{11... | collective-permute-start | bytes 1572872 | tf_op jit(solution)/shard_map/while/body/eval_jaxpr/ppermute | solution.py:11
  403.0 13.1 collective-permute-start
  416.2 34.6 %collective-permute-start = (bf16[128,2,1024]{2,0,1:T(8,128)(2,1)S(1)}, bf16[128,2,1024]{2,0,1:T(8,128)(2,1)S(1)}, u32[]{:S(2)}, u32[]{:S(2)}) collective-permute-start(bf16[128,2,1024]{2,0,1:T(8,128)(2,1)S(1)} %convert_element_type.40), channel_id=1, source_target_pairs={{0,1},{1,2},{2,3},{3,4},{4,5},{5,6},{6,7},{8,9},{9,10},{10,11},{11... | collective-permute-start | bytes 1572872 | tf_op jit(solution)/shard_map/while/body/eval_jaxpr/ppermute | solution.py:11
  450.8 11.5 collective-permute-start
  462.4 34.7 %collective-permute-start = (bf16[128,2,1024]{2,0,1:T(8,128)(2,1)S(1)}, bf16[128,2,1024]{2,0,1:T(8,128)(2,1)S(1)}, u32[]{:S(2)}, u32[]{:S(2)}) collective-permute-start(bf16[128,2,1024]{2,0,1:T(8,128)(2,1)S(1)} %convert_element_type.40), channel_id=1, source_target_pairs={{0,1},{1,2},{2,3},{3,4},{4,5},{5,6},{6,7},{8,9},{9,10},{10,11},{11... | collective-permute-start | bytes 1572872 | tf_op jit(solution)/shard_map/while/body/eval_jaxpr/ppermute | solution.py:11
  497.1 310.7 %copy-start = (bf16[128,1,2,1024]{3,2,1,0:T(2,128)(2,1)S(1)}, bf16[128,1,2,1024]{3,2,1,0:T(2,128)(2,1)}, u32[]{:S(2)}) copy-start(bf16[128,1,2,1024]{3,2,1,0:T(2,128)(2,1)} %param.19) | copy-start | bytes 1572868
  807.8 753.3 %copy-start.1 = (f32[128,2,128]{2,1,0:T(2,128)S(1)}, f32[128,2,128]{2,1,0:T(2,128)}, u32[]{:S(2)}) copy-start(f32[128,2,128]{2,1,0:T(2,128)} %param.18) | copy-start | bytes 393220
  809.1 752.1 %all-reduce.2.cloned.1.call-start = ((), (), s32[]{:S(2)}) async-start(), calls=%async_computation.3 | async-start | bytes 131072 | tf_op jit(solution)/shard_map/psum | solution.py:80
Sparse Core Ops, SparseCore 0:
  12.4 136.3 all-gather.4
  153.3 122.5 all-gather.2
  809.2 626.5 reduce-scatter.3
  1439.4 121.7 all-reduce.1
where the time goes:
time: 1570 us
  waiting for transfers between devices  1090 us (69%)
  local copies, waits for them, and re-layouts  332 us (21%)
  starting transfers between devices  124 us (8%)
    unnamed x5, waiting for transfers between devices  625 us
    gather x1, local copies, waits for them, and re-layouts, per_device(): values = jnp.take_along_axis(current, index_both, axis=2)  311 us
    all_gather x1, waiting for transfers between devices, per_device(): lax.all_gather(lower_inverse, 'src', axis=1, tiled=True)  137 us
    all_gather x1, waiting for transfers between devices, per_device(): lax.all_gather(coupling, 'src', axis=1, tiled=True)  127 us
    psum x1, waiting for transfers between devices, per_device(): picked = lax.psum(values.astype(jnp.bfloat16), 'fac').astype(jnp.float32)  124 us
    ppermute x8, starting transfers between devices, from_behind(): return lax.ppermute(shard, axis, pairs)  124 us
    ppermute x8, waiting for transfers between devices, from_behind(): return lax.ppermute(shard, axis, pairs)  73 us
  transfers between devices with their start and end apart: 12, of which 12 were waited for; matrix products, arithmetic and copies ran while one was open for 0% of the time, Pallas kernels for 0%

commit v1 on v0

--- a/solution.py
+++ b/solution.py
@@ -77,7 +77,9 @@
     index_both = jnp.broadcast_to(clipped[:, None, :], observed.shape)
     values = jnp.take_along_axis(current, index_both, axis=2)
     values = jnp.where(inside[:, None, :], values, jnp.zeros((), jnp.float32))
-    picked = lax.psum(values.astype(jnp.bfloat16), "fac").astype(jnp.float32)
+    picked = jnp.sum(lax.all_gather(values.astype(jnp.bfloat16), axis_name="fac"), 0).astype(
+        jnp.float32
+    )
     scale = 1.0 / math.sqrt(sources * lax.axis_size("src"))
     terms = jnp.sum(current * adjoint[:, 0].astype(jnp.float32), axis=(0, 1)) * scale
     gradient = lax.psum_scatter(terms[None, :], "src", scatter_dimension=1, tiled=True)

time: 1570 us -> 1510 us (0.962)
  the two profiles are of different devices: /device:TPU:2 before, /device:TPU:32 now
where the time goes in v1:
time: 1510 us; the launch traced here: 1500 us
  waiting for transfers between devices  931 us (62%)
  local copies, waits for them, and re-layouts  333 us (22%)
  blocking collectives  117 us (8%)
  starting transfers between devices  98.4 us (7%)
    unnamed x4, waiting for transfers between devices  566 us
    gather x1, local copies, waits for them, and re-layouts, per_device(): values = jnp.take_along_axis(current, index_both, axis=2)  311 us
    all_gather x1, waiting for transfers between devices, per_device(): lax.all_gather(lower_inverse, 'src', axis=1, tiled=True)  132 us
    all_gather x1, waiting for transfers between devices, per_device(): lax.all_gather(coupling, 'src', axis=1, tiled=True)  127 us
    all_gather x1, blocking collectives, per_device(): lax.all_gather(values.astype(jnp.bfloat16), axis_name='fac')  117 us
    ppermute x8, waiting for transfers between devices, from_behind(): return lax.ppermute(shard, axis, pairs)  107 us
    ppermute x8, starting transfers between devices, from_behind(): return lax.ppermute(shard, axis, pairs)  98.3 us
  transfers between devices with their start and end apart: 11, of which 11 were waited for; matrix products, arithmetic and copies ran while one was open for 0% of the time, Pallas kernels for 0%

profile of v1, /device:TPU:32, one launch (start us, length us, event | category | flops | bytes accessed | tf_op | source)
XLA Modules:
  0.0 1504.8 jit_solution(6021189464388300669)
XLA Ops:
  7.2 0.7 all-gather.5.cloned.1.call-update
  7.9 0.7 all-gather.3.cloned.1.call-update
  8.7 1.1 copy.34
  9.9 0.9 broadcast_add_fusion
  10.7 0.9 compare_and_fusion
  11.6 0.2 shift-left_or_fusion
  11.8 131.5 %all-gather.5.cloned.1.call-done = bf16[1,1024,2,1024]{3,2,0,1:T(2,128)(2,1)} async-done(((bf16[1,16,2,1024]{3,2,0,1:T(2,128)(2,1)}), bf16[1,1024,2,1024]{3,2,0,1:T(2,128)(2,1)}) %all-gather.5.cloned.1.call-update) | async-done | bytes 4194320 | tf_op jit(solution)/shard_map/all_gather | solution.py:53
  143.3 127.0 %all-gather.3.cloned.1.call-done = bf16[1,1024,2,1024]{3,2,0,1:T(2,128)(2,1)} async-done(((bf16[1,16,2,1024]{3,2,0,1:T(2,128)(2,1)}), bf16[1,1024,2,1024]{3,2,0,1:T(2,128)(2,1)}) %all-gather.3.cloned.1.call-update) | async-done | bytes 4194320 | tf_op jit(solution)/shard_map/all_gather | solution.py:54
  270.3 0.1 broadcast_in_dim.64
  270.4 229.8 %while.18 = (s32[]{:T(128)}, f32[128,2,1024]{2,0,1:T(8,128)S(1)}, bf16[128,2,1024]{2,0,1:T(8,128)(2,1)S(1)}, s32[]{:T(128)}, s32[128]{0:T(128)}, /*index=5*/f32[...) while((s32[]{:T(128)}, f32[128,2,1024]{2,0,1:T(8,128)S(1)}, ...), condition=%wide.region_3.4_spmd, body=%wide.region_0.3_spmd.sunk | while | flops 2154169344 | bytes 39597816 | solution.py:73
  270.4 0.1 convert_element_type.49
  270.5 2.0 collective-permute-start
  272.6 42.2 %collective-permute-done = bf16[128,2,1024]{2,0,1:T(8,128)(2,1)S(1)} collective-permute-done((bf16[128,2,1024]{2,0,1:T(8,128)(2,1)S(1)}, bf16[128,2,1024]{2,0,1:T(8,128)(2,1)S(1)}, u32[]{:S(2)}, u32[]{:S(2)}) %collective-permute-start) | collective-permute-done | bytes 524320 | tf_op jit(solution)/shard_map/while/body/eval_jaxpr/ppermute | solution.py:11
  314.8 23.8 %conditional.2 = (f32[128,2,1024]{2,0,1:T(8,128)S(1)}) conditional(s32[]{:T(128)} %convert_element_type.48, f32[128,2,1024]{2,0,1:T(8,128)S(1)} %get-tuple-element.299, (s32[128]{0:T(128)}, s32[]{:T(128)}, f32[128,2]{0,1:T(2,128)}, bf16[128,2,1024]{2,0,1:T(8,128)(2,1)S(1)}, bf16[1,1024,2,1024]{3,2,1,0:T(2,128)(2,1)}, ...), branch_computations={%region_1.0_spmd, %region_2.2_spmd} | conditional | flops 2153907200 | bytes 35927604 | solution.py:69
  314.8 0.8 broadcast_compare_fusion
  315.6 0.1 maximum_bitcast_fusion
  315.7 7.8 reshape.97
  323.6 3.5 fusion
  327.1 0.1 maximum_bitcast_fusion.2
  327.2 7.8 reshape.98
  335.0 3.5 fusion.4
  338.5 0.1 convert_element_type.49
  338.6 1.9 collective-permute-start
  340.5 13.6 collective-permute-done
  354.1 0.1 convert_element_type.49
  354.2 26.0 %collective-permute-start = (bf16[128,2,1024]{2,0,1:T(8,128)(2,1)S(1)}, bf16[128,2,1024]{2,0,1:T(8,128)(2,1)S(1)}, u32[]{:S(2)}, u32[]{:S(2)}) collective-permute-start(bf16[128,2,1024]{2,0,1:T(8,128)(2,1)S(1)} %convert_element_type.49), channel_id=1, source_target_pairs={{0,1},{1,2},{2,3},{3,4},{4,5},{5,6},{6,7},{8,9},{9,10},{10,11},{11... | collective-permute-start | bytes 1572872 | tf_op jit(solution)/shard_map/while/body/eval_jaxpr/ppermute | solution.py:11
  380.2 10.5 collective-permute-done
  390.8 4.4 collective-permute-start
  395.2 9.6 collective-permute-done
  404.8 0.1 convert_element_type.49
  404.8 26.2 %collective-permute-start = (bf16[128,2,1024]{2,0,1:T(8,128)(2,1)S(1)}, bf16[128,2,1024]{2,0,1:T(8,128)(2,1)S(1)}, u32[]{:S(2)}, u32[]{:S(2)}) collective-permute-start(bf16[128,2,1024]{2,0,1:T(8,128)(2,1)S(1)} %convert_element_type.49), channel_id=1, source_target_pairs={{0,1},{1,2},{2,3},{3,4},{4,5},{5,6},{6,7},{8,9},{9,10},{10,11},{11... | collective-permute-start | bytes 1572872 | tf_op jit(solution)/shard_map/while/body/eval_jaxpr/ppermute | solution.py:11
  431.1 9.0 collective-permute-done
  440.1 4.4 collective-permute-start
  444.5 8.0 collective-permute-done
  452.7 27.7 %collective-permute-start = (bf16[128,2,1024]{2,0,1:T(8,128)(2,1)S(1)}, bf16[128,2,1024]{2,0,1:T(8,128)(2,1)S(1)}, u32[]{:S(2)}, u32[]{:S(2)}) collective-permute-start(bf16[128,2,1024]{2,0,1:T(8,128)(2,1)S(1)} %convert_element_type.49), channel_id=1, source_target_pairs={{0,1},{1,2},{2,3},{3,4},{4,5},{5,6},{6,7},{8,9},{9,10},{10,11},{11... | collective-permute-start | bytes 1572872 | tf_op jit(solution)/shard_map/while/body/eval_jaxpr/ppermute | solution.py:11
  480.4 7.4 collective-permute-done
  487.9 5.6 collective-permute-start
  493.5 6.7 collective-permute-done
  500.2 310.7 %gather_fusion = bf16[32768]{0:T(1024)(128)(2,1)S(1)} fusion(f32[128,2,1024]{2,0,1:T(8,128)S(1)} %get-tuple-element.168, s32[32768]{0:T(1024)S(1)} %bitcast.37), kind=kCustom, calls=%fused_computation | custom fusion | bytes 524288 | tf_op jit(solution)/shard_map/jit(take_along_axis)/gather | solution.py:78
  810.9 0.2 fusion.14
  811.1 0.2 fusion.12
  811.4 117.3 %all_gather.12 = bf16[8,128,2,128]{3,1,2,0:T(8,128)(2,1)S(1)} all-gather(bf16[1,128,2,128]{3,1,2,0:T(8,128)(2,1)S(1)} %copy.38), channel_id=1, replica_groups=mesh['src'=64,'fac'=8] {'fac'}, dimensions={0}, use_global_device_ids=true | all-gather | bytes 589824 | tf_op jit(solution)/shard_map/all_gather | solution.py:80
  928.7 1.0 copy.42
  929.7 0.1 reduce_sum.21
  929.8 1.8 copy.47
  931.6 0.8 copy.41
  932.4 564.6 %reduce-scatter.4.cloned.1.call-done = f32[16,1]{1,0:T(8,128)} async-done(((f32[1024,1]{1,0:T(8,128)}), f32[16,1]{1,0:T(8,128)}) %reduce-scatter.4.cloned.1.call-update) | async-done | bytes 80
  1497.0 1.3 copy.43
  (29 shorter events, 0.6 us)
Async XLA Ops:
  7.2 136.1 %all-gather.5.cloned.1.call-start = ((), (), s32[]{:S(2)}) async-start(), calls=%async_computation.2 | async-start | bytes 4259840 | tf_op jit(solution)/shard_map/all_gather | solution.py:53
  7.9 262.4 %all-gather.3.cloned.1.call-start = ((), (), s32[]{:S(2)}) async-start(), calls=%async_computation.1 | async-start | bytes 4259840 | tf_op jit(solution)/shard_map/all_gather | solution.py:54
  8.6 1488.4 %reduce-scatter.4.cloned.1.call-start = ((), (), s32[]{:S(2)}) async-start(), calls=%async_computation.3 | async-start | bytes 532480
  270.5 44.2 %collective-permute-start = (bf16[128,2,1024]{2,0,1:T(8,128)(2,1)S(1)}, bf16[128,2,1024]{2,0,1:T(8,128)(2,1)S(1)}, u32[]{:S(2)}, u32[]{:S(2)}) collective-permute-start(bf16[128,2,1024]{2,0,1:T(8,128)(2,1)S(1)} %convert_element_type.49), channel_id=1, source_target_pairs={{0,1},{1,2},{2,3},{3,4},{4,5},{5,6},{6,7},{8,9},{9,10},{10,11},{11... | collective-permute-start | bytes 1572872 | tf_op jit(solution)/shard_map/while/body/eval_jaxpr/ppermute | solution.py:11
  315.7 7.8 copy-start.2
  338.6 15.5 %collective-permute-start = (bf16[128,2,1024]{2,0,1:T(8,128)(2,1)S(1)}, bf16[128,2,1024]{2,0,1:T(8,128)(2,1)S(1)}, u32[]{:S(2)}, u32[]{:S(2)}) collective-permute-start(bf16[128,2,1024]{2,0,1:T(8,128)(2,1)S(1)} %convert_element_type.49), channel_id=1, source_target_pairs={{0,1},{1,2},{2,3},{3,4},{4,5},{5,6},{6,7},{8,9},{9,10},{10,11},{11... | collective-permute-start | bytes 1572872 | tf_op jit(solution)/shard_map/while/body/eval_jaxpr/ppermute | solution.py:11
  354.2 36.5 %collective-permute-start = (bf16[128,2,1024]{2,0,1:T(8,128)(2,1)S(1)}, bf16[128,2,1024]{2,0,1:T(8,128)(2,1)S(1)}, u32[]{:S(2)}, u32[]{:S(2)}) collective-permute-start(bf16[128,2,1024]{2,0,1:T(8,128)(2,1)S(1)} %convert_element_type.49), channel_id=1, source_target_pairs={{0,1},{1,2},{2,3},{3,4},{4,5},{5,6},{6,7},{8,9},{9,10},{10,11},{11... | collective-permute-start | bytes 1572872 | tf_op jit(solution)/shard_map/while/body/eval_jaxpr/ppermute | solution.py:11
  390.8 14.0 collective-permute-start
  404.8 35.2 %collective-permute-start = (bf16[128,2,1024]{2,0,1:T(8,128)(2,1)S(1)}, bf16[128,2,1024]{2,0,1:T(8,128)(2,1)S(1)}, u32[]{:S(2)}, u32[]{:S(2)}) collective-permute-start(bf16[128,2,1024]{2,0,1:T(8,128)(2,1)S(1)} %convert_element_type.49), channel_id=1, source_target_pairs={{0,1},{1,2},{2,3},{3,4},{4,5},{5,6},{6,7},{8,9},{9,10},{10,11},{11... | collective-permute-start | bytes 1572872 | tf_op jit(solution)/shard_map/while/body/eval_jaxpr/ppermute | solution.py:11
  440.1 12.4 collective-permute-start
  452.7 35.1 %collective-permute-start = (bf16[128,2,1024]{2,0,1:T(8,128)(2,1)S(1)}, bf16[128,2,1024]{2,0,1:T(8,128)(2,1)S(1)}, u32[]{:S(2)}, u32[]{:S(2)}) collective-permute-start(bf16[128,2,1024]{2,0,1:T(8,128)(2,1)S(1)} %convert_element_type.49), channel_id=1, source_target_pairs={{0,1},{1,2},{2,3},{3,4},{4,5},{5,6},{6,7},{8,9},{9,10},{10,11},{11... | collective-permute-start | bytes 1572872 | tf_op jit(solution)/shard_map/while/body/eval_jaxpr/ppermute | solution.py:11
  487.9 12.3 collective-permute-start
  500.2 311.0 %copy-start = (bf16[128,1,2,1024]{3,2,1,0:T(2,128)(2,1)S(1)}, bf16[128,1,2,1024]{3,2,1,0:T(2,128)(2,1)}, u32[]{:S(2)}) copy-start(bf16[128,1,2,1024]{3,2,1,0:T(2,128)(2,1)} %param.19) | copy-start | bytes 1572868
  810.9 119.0 %copy-start.1 = (f32[128,2,128]{2,1,0:T(2,128)S(1)}, f32[128,2,128]{2,1,0:T(2,128)}, u32[]{:S(2)}) copy-start(f32[128,2,128]{2,1,0:T(2,128)} %param.18) | copy-start | bytes 393220
Sparse Core Ops, SparseCore 0:
  12.4 130.8 all-gather.4
  147.7 122.5 all-gather.2
  929.9 567.1 reduce-scatter.3
